TPU v7x, 128 devices: a whole 4x4x4 slice. The times are simulated.
128 devices in a mesh: group: 8 (over z_lo, x), shard: 16 (over z_hi, y, core).
Axes of the slice: x: 4, y: 4, z: 4 (z_hi: 2, z_lo: 2; z = z_hi * 2 + z_lo), core: 2. Of those that a mesh axis runs over, the one named last changes fastest.
Arguments:
- src_emb: float32 [400, 262144], P(None, ('group', 'shard')), may hold values from -1.5 to 1.5
- src_state: float32 [262144], P(('group', 'shard')), may hold values from 0.1 to 1
- dst_emb: float32 [400, 8192], P(None, ('group', 'shard')), may hold values from -1.5 to 1.5
- dst_state: float32 [8192], P(('group', 'shard')), may hold values from 100 to 10000
- rel_table: float32 [400, 64], replicated, may hold values from -3 to 3
- rel_ids: int32 [2, 2, 8, 4], P(None, None, 'group'), may hold values from 0 to 63
- multiplicity: int32 [2, 2, 2048, 4], P(None, None, ('group', 'shard')), may hold values from 0 to 2
- neg_tile: int32 [2, 2, 2048], P(None, None, ('group', 'shard')), may hold values from 0 to 3
Outputs:
- src_out: float32 [400, 262144], P(None, ('group', 'shard'))
- src_state_out: float32 [262144], P(('group', 'shard'))
- dst_out: float32 [400, 8192], P(None, ('group', 'shard'))
- dst_state_out: float32 [8192], P(('group', 'shard'))
All inputs are finite; a program needn't handle non-finite values.
Results may differ from a plain program's by a relative error of at most 0.0004.
The roundings to bfloat16 on the way count: a program that leaves them out, or rounds other values in their place, can miss the bound.
Values may be sent and summed in bfloat16 or wider, within the bound.
No kernel may reach another device: no remote copies, remote signals or barrier semaphores. Data moves between devices by JAX's collectives and lax.ppermute only.
A program may use at most 64 MiB of HBM per device.

v0:
```python
import jax
import jax.numpy as jnp
from jax import lax
from jax.sharding import PartitionSpec as P

POOLS = 2
ROUNDS = 2
TILE = 128
LEARN_RATE = 0.1
POSITIVE_WEIGHT = 0.125
NEGATIVE_WEIGHT = 0.25
HIGHEST_PRECISION = lax.Precision.HIGHEST


def from_behind(value, axis, steps):
    count = lax.axis_size(axis)
    pairs = [(source, (source + steps) % count) for source in range(count)]
    return lax.ppermute(value, axis, pairs)


def column_tiles(offset, columns, tile_count):
    tile_of = (offset + lax.iota(jnp.int32, columns)) // TILE
    return (tile_of[None, :] == lax.iota(jnp.int32, tile_count)[:, None]).astype(jnp.float32)


def relation_columns(rel_table, rel_row, offset, columns):
    tile_count = rel_row.shape[0]
    chosen = (rel_row[None, :] == lax.iota(jnp.int32, rel_table.shape[1])[:, None]).astype(
        jnp.float32
    )
    per_tile = jnp.dot(rel_table, chosen, precision=HIGHEST_PRECISION)
    return jnp.dot(per_tile, column_tiles(offset, columns, tile_count), precision=HIGHEST_PRECISION)


def pair_gradient(scores, mult_f, neg_hot, offset, columns):
    col_tiles = column_tiles(offset, columns, mult_f.shape[1])
    positive = jnp.dot(mult_f, col_tiles, precision=HIGHEST_PRECISION)
    negative = jnp.dot(neg_hot, col_tiles, precision=HIGHEST_PRECISION)
    row_tiles = mult_f.shape[0]
    blocked = scores.reshape(row_tiles, TILE, columns)
    pair_grad = NEGATIVE_WEIGHT * negative[:, None, :] * jax.nn.sigmoid(
        blocked
    ) - POSITIVE_WEIGHT * positive[:, None, :] * jax.nn.sigmoid(-blocked)
    return pair_grad.reshape(row_tiles * TILE, columns).astype(jnp.bfloat16)


def adagrad(embedding, accum, gradient):
    new_accum = accum + jnp.mean(gradient * gradient, axis=0)
    return (embedding - LEARN_RATE * gradient / jnp.sqrt(new_accum)[None, :], new_accum)


def local(src_emb, src_state, dst_emb, dst_state, rel_table, rel_ids, multiplicity, neg_tile):
    pool_dev = dst_emb.shape[1] // POOLS
    shard_pos = lax.axis_index("shard")
    pool_cols = pool_dev * lax.axis_size("shard")
    tile_count = multiplicity.shape[3]
    for rotation in range(ROUNDS):
        if rotation > 0:
            dst_emb, dst_state = from_behind((dst_emb, dst_state), "group", 1)
        new_embs = []
        new_sums = []
        for pool_index in range(POOLS):
            local_pool = dst_emb[:, pool_index * pool_dev : (pool_index + 1) * pool_dev]
            local_sums = dst_state[pool_index * pool_dev : (pool_index + 1) * pool_dev]
            rel_row = rel_ids[rotation, pool_index, 0]
            mult_f = multiplicity[rotation, pool_index].astype(jnp.float32)
            neg_hot = (
                neg_tile[rotation, pool_index][:, None] == lax.iota(jnp.int32, tile_count)[None, :]
            ).astype(jnp.float32)
            own_scale = relation_columns(rel_table, rel_row, shard_pos * pool_dev, pool_dev)
            source_bf = src_emb.astype(jnp.bfloat16)
            gathered = lax.all_gather(local_pool, "shard", axis=1, tiled=True)
            scaled = (gathered * relation_columns(rel_table, rel_row, 0, pool_cols)).astype(
                jnp.bfloat16
            )
            scores = lax.dot_general(
                source_bf, scaled, (((0,), (0,)), ((), ())), preferred_element_type=jnp.float32
            )
            pair_grad = pair_gradient(scores, mult_f, neg_hot, 0, pool_cols)
            src_grad = lax.dot_general(
                scaled, pair_grad, (((1,), (1,)), ((), ())), preferred_element_type=jnp.float32
            )
            src_emb, src_state = adagrad(src_emb, src_state, src_grad)
            dest_part = jnp.dot(source_bf, pair_grad, preferred_element_type=jnp.float32)
            summed = lax.psum_scatter(dest_part, "shard", scatter_dimension=1, tiled=True)
            updated, updated_sums = adagrad(local_pool, local_sums, own_scale * summed)
            new_embs.append(updated)
            new_sums.append(updated_sums)
        dst_emb = jnp.concatenate(new_embs, axis=1)
        dst_state = jnp.concatenate(new_sums, axis=0)
    dst_emb, dst_state = from_behind((dst_emb, dst_state), "group", 1 - ROUNDS)
    return (src_emb, src_state, dst_emb, dst_state)


def solution(mesh):
    placed = (
        P(None, ("group", "shard")),
        P(("group", "shard")),
        P(None, ("group", "shard")),
        P(("group", "shard")),
        P(),
        P(None, None, "group", None),
        P(None, None, ("group", "shard"), None),
        P(None, None, ("group", "shard")),
    )
    return jax.shard_map(
        local,
        mesh=mesh,
        in_specs=placed,
        out_specs=(
            P(None, ("group", "shard")),
            P(("group", "shard")),
            P(None, ("group", "shard")),
            P(("group", "shard")),
        ),
        check_vma=False,
    )
```

profile of v0, /device:TPU:0, one launch (start us, length us, event | category | flops | bytes accessed | tf_op | source)
XLA Modules:
  0.0 458.4 jit_solution(17057751256044241185)
XLA Ops:
  8.1 0.9 fusion.12
  10.6 28.3 %all_gather.12 = f32[400,512]{0,1:T(8,128)S(1)} all-gather(f32[400,32]{0,1:T(8,128)S(1)} %get-tuple-element.27), channel_id=1, replica_groups=mesh['group'=8,'shard'=16] {'shard'}, dimensions={1}, use_global_device_ids=true | all-gather | bytes 870400 | tf_op jit(solution)/shard_map/all_gather | solution.py:72
  41.0 1.1 mul.212
  42.1 1.1 mul.217
  44.1 5.4 %fusion.1 = bf16[2048,512]{0,1:T(8,128)(2,1)S(1)} fusion(f32[64,8,16,128]{3,2,1,0:T(8,128)S(1)} %bitcast.133, f32[64,8,16,128]{3,2,1,0:T(8,128)S(1)} %bitcast.132, bf16[400,512]{1,0:T(8,128)(2,1)S(1)} %fusion.8, f32[400,2048]{1,0:T(8,128)S(1)} %copy-done.9), kind=kOutput, calls=%fused_computation.2 | convolution fusion | flops 849117184 | bytes 14172160 | tf_op jit(solution)/shard_map/dot_general | solution.py:76
  49.5 1.0 multiply_reduce_fusion.3
  51.0 23.7 %all_gather.13 = f32[400,512]{0,1:T(8,128)} all-gather(f32[400,32]{0,1:T(8,128)S(1)} %get-tuple-element.26), channel_id=1, replica_groups=mesh['group'=8,'shard'=16] {'shard'}, dimensions={1}, use_global_device_ids=true | all-gather | bytes 870400 | tf_op jit(solution)/shard_map/all_gather | solution.py:72
  74.8 2.4 copy.27
  77.4 2.7 divide_subtract_fusion.3
  80.7 3.2 fusion.7
  83.9 2.3 convolution_bitcast_fusion.2
  86.5 3.6 convolution_bitcast_fusion.3
  90.1 1.3 copy.40
  91.5 2.7 multiply_reduce_fusion.2
  96.1 1.5 fusion.37
  99.8 1.5 fusion.36
  101.2 3.7 divide_subtract_fusion.2
  105.0 46.3 %reduce-scatter.15.cloned.1.call-done = f32[32,400]{1,0:T(8,128)} async-done(((f32[512,400]{1,0:T(8,128)}), f32[32,400]{1,0:T(8,128)}) %reduce-scatter.15.cloned.1.call-update) | async-done | bytes 51216
  151.3 2.3 multiply_reduce_fusion.6
  153.6 67.5 %reduce-scatter.13.cloned.1.call-done = f32[32,400]{1,0:T(8,128)} async-done(((f32[512,400]{1,0:T(8,128)}), f32[32,400]{1,0:T(8,128)}) %reduce-scatter.13.cloned.1.call-update) | async-done | bytes 51216
  221.1 1.2 multiply_reduce_fusion.7
  222.3 1.3 fusion.78
  223.6 0.9 divide_subtract_fusion.7
  224.6 1.6 collective-permute-start
  226.1 1.5 convolution_multiply_fusion.7
  227.6 4.1 collective-permute-done
  232.3 25.8 %all_gather.14 = f32[400,512]{0,1:T(8,128)} all-gather(f32[400,32]{0,1:T(8,128)S(1)} %get-tuple-element.23), channel_id=1, replica_groups=mesh['group'=8,'shard'=16] {'shard'}, dimensions={1}, use_global_device_ids=true | all-gather | bytes 870400 | tf_op jit(solution)/shard_map/all_gather | solution.py:72
  258.2 2.4 copy.31
  260.6 1.5 multiply_convert_fusion.1
  262.1 4.0 fusion.5
  266.1 3.3 multiply_reduce_fusion.1
  269.4 22.3 %all_gather.15 = f32[400,512]{0,1:T(8,128)S(1)} all-gather(f32[400,32]{0,1:T(8,128)S(1)} %copy-done.12), channel_id=1, replica_groups=mesh['group'=8,'shard'=16] {'shard'}, dimensions={1}, use_global_device_ids=true | all-gather | bytes 870400 | tf_op jit(solution)/shard_map/all_gather | solution.py:72
  291.7 1.2 copy.32
  293.7 3.7 divide_subtract_fusion.1
  298.4 3.2 fusion.3
  301.6 1.3 copy-done.4
  303.0 2.3 convolution_bitcast_fusion
  305.6 4.9 %convolution_bitcast_fusion.1 = f32[512,400]{1,0:T(8,128)} fusion(bf16[2048,512]{1,0:T(8,128)(2,1)} %copy-done.3, f32[400,2048]{1,0:T(8,128)} %copy-done.1), kind=kOutput, calls=%fused_computation.25 | convolution fusion | flops 839680000 | bytes 6193152
  310.5 1.2 pad_maximum_fusion.2
  311.7 4.5 multiply_reduce_fusion
  316.8 53.0 %reduce-scatter.19.cloned.1.call-done = f32[32,400]{1,0:T(8,128)} async-done(((f32[512,400]{1,0:T(8,128)}), f32[32,400]{1,0:T(8,128)}) %reduce-scatter.19.cloned.1.call-update) | async-done | bytes 51216
  369.9 2.3 multiply_reduce_fusion.4
  372.2 67.4 %reduce-scatter.17.cloned.1.call-done = f32[32,400]{1,0:T(8,128)} async-done(((f32[512,400]{1,0:T(8,128)}), f32[32,400]{1,0:T(8,128)}) %reduce-scatter.17.cloned.1.call-update) | async-done | bytes 51216
  439.5 1.2 multiply_reduce_fusion.5
  441.6 2.9 collective-permute-start.3
  444.5 0.9 divide_subtract_fusion.5
  445.4 0.9 collective-permute-start.2
  446.4 4.3 divide_subtract_fusion
  (91 shorter events, 16.2 us)
Async XLA Ops:
  7.2 33.0 %copy-start = (f32[400,64]{0,1:T(8,128)S(1)}, f32[400,64]{0,1:T(8,128)}, u32[]{:S(2)}) copy-start(f32[400,64]{0,1:T(8,128)} %param.12) | copy-start | bytes 307204
  7.2 32.0 %copy-start.21 = (s32[2,2,16]{2,1,0:T(2,128)S(1)}, s32[2,2,16]{2,1,0:T(2,128)}, u32[]{:S(2)}) copy-start(s32[2,2,16]{2,1,0:T(2,128)} %param.15) | copy-start | bytes 772
  7.2 144.1 %reduce-scatter.15.cloned.1.call-start = ((), (), s32[]{:S(2)}) async-start(), calls=%async_computation.5 | async-start | bytes 1114112
  7.2 92.5 %copy-start.17 = (s32[512]{0:T(512)}, s32[512]{0:T(512)S(1)}, u32[]{:S(2)}) copy-start(s32[512]{0:T(512)S(1)} %add_select_fusion) | copy-start | bytes 6148
  40.4 2.9 copy-start.13
  42.1 1.9 copy-start.9
  49.5 1.3 copy-start.10
  49.5 27.7 %copy-start.22 = (s32[16]{0:T(128)S(1)}, s32[16]{0:T(128)}, u32[]{:S(2)}) copy-start(s32[16]{0:T(128)} %get-tuple-element.29) | copy-start | bytes 196
  49.5 27.8 %copy-start.20 = (f32[2048]{0:T(1024)S(1)}, f32[2048]{0:T(1024)}, u32[]{:S(2)}) copy-start(f32[2048]{0:T(1024)} %param.9) | copy-start | bytes 24580
  51.0 29.1 %copy-start.14 = (f32[4,400]{1,0:T(4,128)}, f32[4,400]{1,0:T(4,128)S(1)}, u32[]{:S(2)}) copy-start(f32[4,400]{1,0:T(4,128)S(1)} %fusion.29) | copy-start | bytes 19204
  77.4 2.7 copy-start.6
  80.1 3.8 copy-start.2
  86.3 134.8 %reduce-scatter.13.cloned.1.call-start = ((), (), s32[]{:S(2)}) async-start(), calls=%async_computation.4 | async-start | bytes 1114112
  91.5 278.4 %reduce-scatter.19.cloned.1.call-start = ((), (), s32[]{:S(2)}) async-start(), calls=%async_computation.7 | async-start | bytes 1114112
  91.5 2.7 copy-start.23
  101.2 122.4 %copy-start.11 = (f32[400,64]{0,1:T(8,128)S(1)}, f32[400,64]{0,1:T(8,128)}, u32[]{:S(2)}) copy-start(f32[400,64]{0,1:T(8,128)} %param.10) | copy-start | bytes 307204
  105.0 161.1 %copy-start.1 = (f32[400,2048]{1,0:T(8,128)}, f32[400,2048]{1,0:T(8,128)S(1)}, u32[]{:S(2)}) copy-start(f32[400,2048]{1,0:T(8,128)S(1)} %divide_subtract_fusion.2) | copy-start | bytes 9830404
  224.6 7.1 %collective-permute-start = (f32[400,64]{0,1:T(8,128)S(1)}, f32[400,64]{0,1:T(8,128)S(1)}, u32[]{:S(2)}, u32[]{:S(2)}) collective-permute-start(f32[400,64]{0,1:T(8,128)S(1)} %pad_maximum_fusion), channel_id=1, source_target_pairs={{0,16},{16,32},{32,48},{48,64},{64,80},{80,96},{96,112},{112,0},{1... | collective-permute-start | bytes 307208 | tf_op jit(solution)/shard_map/ppermute | solution.py:18
  266.1 3.3 copy-start.3
  266.1 3.3 copy-start.12
  293.7 3.8 copy-start.7
  293.7 3.8 copy-start.8
  293.7 4.7 %copy-start.18 = (f32[16,512]{1,0:T(8,128)S(1)}, f32[16,512]{1,0:T(8,128)}, u32[]{:S(2)}) copy-start(f32[16,512]{1,0:T(8,128)} %fusion.10) | copy-start | bytes 98308
  293.7 4.7 %copy-start.19 = (f32[16,512]{1,0:T(8,128)S(1)}, f32[16,512]{1,0:T(8,128)}, u32[]{:S(2)}) copy-start(f32[16,512]{1,0:T(8,128)} %convolution_multiply_fusion.7) | copy-start | bytes 98308
  297.7 0.8 copy-start.5
  301.6 1.3 copy-start.4
  305.3 134.3 %reduce-scatter.17.cloned.1.call-start = ((), (), s32[]{:S(2)}) async-start(), calls=%async_computation.6 | async-start | bytes 1114112
  311.7 4.6 copy-start.15
  311.7 4.6 copy-start.16
  311.7 129.0 %collective-permute-start.1 = (f32[64]{0:T(128)}, f32[64]{0:T(128)}, u32[]{:S(2)}, u32[]{:S(2)}) collective-permute-start(f32[64]{0:T(128)} %pad_maximum_fusion.2), channel_id=1, source_target_pairs={{0,16},{16,32},{32,48},{48,64},{64,80},{80,96},{96,112},{112,0},{1... | collective-permute-start | bytes 776 | tf_op jit(solution)/shard_map/ppermute | solution.py:18
  441.6 9.1 %collective-permute-start.3 = (f32[64]{0:T(128)S(1)}, f32[64]{0:T(128)S(1)}, u32[]{:S(2)}, u32[]{:S(2)}) collective-permute-start(f32[64]{0:T(128)S(1)} %pad_maximum_fusion.3), channel_id=1, source_target_pairs={{0,112},{16,0},{32,16},{48,32},{64,48},{80,64},{96,80},{112,96},{1... | collective-permute-start | bytes 776 | tf_op jit(solution)/shard_map/ppermute | solution.py:18
  445.4 5.2 %collective-permute-start.2 = (f32[400,64]{0,1:T(8,128)S(1)}, f32[400,64]{0,1:T(8,128)S(1)}, u32[]{:S(2)}, u32[]{:S(2)}) collective-permute-start(f32[400,64]{0,1:T(8,128)S(1)} %pad_maximum_fusion.1), channel_id=1, source_target_pairs={{0,112},{16,0},{32,16},{48,32},{64,48},{80,64},{96,80},{112,96},{1... | collective-permute-start | bytes 307208 | tf_op jit(solution)/shard_map/ppermute | solution.py:18
Sparse Core Ops, SparseCore 0:
  86.4 64.8 reduce-scatter.14
  155.1 65.9 reduce-scatter.12
  305.4 64.4 reduce-scatter.18
  373.6 65.9 reduce-scatter.16
where the time goes:
time: 459 us; the launch traced here: 458 us
  waiting for transfers between devices  238 us (52%)
  blocking collectives  100 us (22%)
  matrix products  58.5 us (13%)
  other arithmetic  24 us (5%)
  local copies, waits for them, and re-layouts  17.4 us (4%)
  between operations  14.2 us (3%)
  starting transfers between devices  5.95 us (1%)
    unnamed x8, waiting for transfers between devices  234 us
    all_gather x4, blocking collectives, local(): gathered = lax.all_gather(local_pool, 'shard', axis=1, tiled=True)  100 us
    sub x6, other arithmetic, adagrad(): embedding - LEARN_RATE * gradient / jnp.sqrt(new_accum)[None, :]  16.3 us
    dot_general x4, matrix products, local(): lax.dot_general(source_bf, scaled, (((0,), (0,)), ((), ())), preferred_el...  15.8 us
    dot_general x4, matrix products, local(): lax.dot_general(scaled, pair_grad, (((1,), (1,)), ((), ())), preferred_el...  11.6 us
    dot_general x8, matrix products, relation_columns(): jnp.dot(per_tile, column_tiles(offset, columns, tile_count), precision=HI...  11.1 us
    unnamed x3, matrix products  9.51 us
  transfers between devices with their start and end apart: 8, of which 5 were waited for; matrix products, arithmetic and copies ran while one was open for 9% of the time, Pallas kernels for 0%

commit v1 on v0

--- a/solution.py
+++ b/solution.py
@@ -69,7 +69,10 @@
             ).astype(jnp.float32)
             own_scale = relation_columns(rel_table, rel_row, shard_pos * pool_dev, pool_dev)
             source_bf = src_emb.astype(jnp.bfloat16)
-            gathered = lax.all_gather(local_pool, "shard", axis=1, tiled=True)
+            peers = lax.axis_size("shard")
+            blocks = jnp.stack([local_pool for _ in range(peers)])
+            blocks = lax.all_to_all(blocks, "shard", split_axis=0, concat_axis=0)
+            gathered = jnp.concatenate(blocks, axis=1)
             scaled = (gathered * relation_columns(rel_table, rel_row, 0, pool_cols)).astype(
                 jnp.bfloat16
             )

time: 459 us -> 409 us (0.89)
  blocking collectives: 100 us -> 0 us
  waiting for transfers between devices: 238 us -> 263 us
  starting transfers between devices: 5.95 us -> 27.5 us
    unnamed x8 -> x4, waiting for transfers between devices: 234 us -> 0.07 us
    reduce_scatter x0 -> x4, waiting for transfers between devices: none -> 230 us  [local(): lax.psum_scatter(dest_part, 'shard', scatter_dimension=1, tiled=True)]
    all_gather x4 -> x0, blocking collectives: 100 us -> none  [local(): gathered = lax.all_gather(local_pool, 'shard', axis=1, tiled=True)]
    all_to_all x0 -> x4, waiting for transfers between devices: none -> 32.5 us  [local(): blocks = lax.all_to_all(blocks, 'shard', split_axis=0, concat_axis=0)]
    all_to_all x0 -> x4, starting transfers between devices: none -> 20.7 us  [local(): blocks = lax.all_to_all(blocks, 'shard', split_axis=0, concat_axis=0)]
    unnamed x3 -> x0, matrix products: 9.51 us -> none
    all_gather x4 -> x0, local copies, waits for them, and re-layouts: 6.39 us -> none  [local(): gathered = lax.all_gather(local_pool, 'shard', axis=1, tiled=True)]
    dot_general x1 -> x4, matrix products: 3.61 us -> 9.17 us  [local(): jnp.dot(source_bf, pair_grad, preferred_element_type=jnp.float32)]
  transfers between devices with their start and end apart: 8 -> 12, of which waited for: 5 -> 9; matrix products, arithmetic and copies ran while one was open for 9% -> 21% of each run, Pallas kernels for 0% -> 0%
where the time goes in v1:
time: 409 us; the launch traced here: 408 us
  waiting for transfers between devices  263 us (64%)
  matrix products  58.6 us (14%)
  starting transfers between devices  27.5 us (7%)
  other arithmetic  24.1 us (6%)
  local copies, waits for them, and re-layouts  20.8 us (5%)
  between operations  14.2 us (3%)
    reduce_scatter x4, waiting for transfers between devices, local(): lax.psum_scatter(dest_part, 'shard', scatter_dimension=1, tiled=True)  230 us
    all_to_all x4, waiting for transfers between devices, local(): blocks = lax.all_to_all(blocks, 'shard', split_axis=0, concat_axis=0)  32.5 us
    all_to_all x4, starting transfers between devices, local(): blocks = lax.all_to_all(blocks, 'shard', split_axis=0, concat_axis=0)  20.7 us
    sub x6, other arithmetic, adagrad(): embedding - LEARN_RATE * gradient / jnp.sqrt(new_accum)[None, :]  18 us
    dot_general x4, matrix products, local(): lax.dot_general(source_bf, scaled, (((0,), (0,)), ((), ())), preferred_el...  15.9 us
    dot_general x4, matrix products, local(): lax.dot_general(scaled, pair_grad, (((1,), (1,)), ((), ())), preferred_el...  15.7 us
    dot_general x8, matrix products, relation_columns(): jnp.dot(per_tile, column_tiles(offset, columns, tile_count), precision=HI...  11.1 us
    dot_general x4, matrix products, local(): jnp.dot(source_bf, pair_grad, preferred_element_type=jnp.float32)  9.17 us
  transfers between devices with their start and end apart: 12, of which 9 were waited for; matrix products, arithmetic and copies ran while one was open for 21% of the time, Pallas kernels for 0%

profile of v1, /device:TPU:0, one launch (start us, length us, event | category | flops | bytes accessed | tf_op | source)
XLA Modules:
  0.0 408.1 jit_solution(5938208853850203609)
XLA Ops:
  9.2 8.0 %all-to-all-start = ((f32[16,400,32]{1,2,0:T(8,128)}), f32[16,400,32]{1,2,0:T(8,128)S(1)}, u32[]{:S(2)}, u32[]{:S(2)}) async-start(f32[16,400,32]{1,2,0:T(8,128)} %stack.8), calls=%async_computation | async-start | bytes 2097152 | tf_op jit(solution)/shard_map/all_to_all | solution.py:74
  21.6 13.6 %all-to-all-done = f32[16,400,32]{1,2,0:T(8,128)S(1)} async-done(((f32[16,400,32]{1,2,0:T(8,128)}), f32[16,400,32]{1,2,0:T(8,128)S(1)}, u32[]{:S(2)}, u32[]{:S(2)}) %all-to-all-start) | async-done | bytes 819232 | tf_op jit(solution)/shard_map/all_to_all | solution.py:74
  35.2 1.1 stack.9
  36.3 3.7 all-to-all-start.1
  40.9 2.1 mul.212
  45.0 5.4 %fusion.1 = bf16[2048,512]{0,1:T(8,128)(2,1)S(1)} fusion(f32[64,8,16,128]{3,2,1,0:T(8,128)S(1)} %bitcast.131, f32[64,8,16,128]{3,2,1,0:T(8,128)S(1)} %bitcast.130, bf16[400,512]{1,0:T(8,128)(2,1)S(1)} %fusion.8, f32[400,2048]{1,0:T(8,128)S(1)} %copy-done.6), kind=kOutput, calls=%fused_computation.2 | convolution fusion | flops 849117184 | bytes 14172160 | tf_op jit(solution)/shard_map/dot_general | solution.py:79
  50.4 2.7 multiply_reduce_fusion.3
  53.1 2.3 convolution_bitcast_fusion
  55.4 2.5 all-to-all-done.1
  59.1 3.7 divide_subtract_fusion.3
  62.8 3.2 fusion.7
  66.1 1.3 copy-done.2
  67.4 2.3 fusion.22
  70.3 1.5 fusion.10
  71.8 1.5 fusion.11
  74.3 50.3 %reduce-scatter.5.cloned.1.call-done = f32[400,32]{0,1:T(8,128)} async-done(((f32[400,512]{0,1:T(8,128)}), f32[400,32]{0,1:T(8,128)}) %reduce-scatter.5.cloned.1.call-update) | async-done | bytes 51216 | tf_op jit(solution)/shard_map/reduce_scatter | solution.py:88
  124.6 2.3 multiply_reduce_fusion.7
  127.0 68.1 %reduce-scatter.7.cloned.1.call-done = f32[400,32]{0,1:T(8,128)} async-done(((f32[400,512]{0,1:T(8,128)}), f32[400,32]{0,1:T(8,128)}) %reduce-scatter.7.cloned.1.call-update) | async-done | bytes 51216 | tf_op jit(solution)/shard_map/reduce_scatter | solution.py:88
  195.0 1.2 multiply_reduce_fusion.6
  196.2 1.4 fusion.81
  198.5 1.5 collective-permute-start
  200.1 5.1 %multiply_reduce_fusion.2 = (f32[2048]{0:T(1024)}, f32[400,2048]{1,0:T(8,128)}) fusion(bf16[400,512]{1,0:T(8,128)(2,1)} %copy-done.4, bf16[2048,512]{1,0:T(8,128)(2,1)} %copy-done.2), kind=kOutput, calls=%fused_computation.21 | convolution fusion | flops 840497152 | bytes 5791744 | tf_op jit(solution)/shard_map/dot_general | solution.py:83
  207.4 4.7 %all-to-all-start.2 = ((f32[16,400,32]{1,2,0:T(8,128)}), f32[16,400,32]{1,2,0:T(8,128)}, u32[]{:S(2)}, u32[]{:S(2)}) async-start(f32[16,400,32]{1,2,0:T(8,128)} %stack.10), calls=%async_computation.4 | async-start | bytes 2097152 | tf_op jit(solution)/shard_map/all_to_all | solution.py:74
  212.1 1.3 fusion.83
  213.5 4.4 %divide_subtract_fusion.2 = f32[400,2048]{1,0:T(8,128)} fusion(f32[400,2048]{1,0:T(8,128)S(1)} %divide_subtract_fusion.3, f32[400,2048]{1,0:T(8,128)} %get-tuple-element.39, f32[2048]{0:T(1024)S(1)} %get-tuple-element.14), kind=kLoop, calls=%fused_computation.20 | loop fusion | flops 2457600 | bytes 9838592 | tf_op jit(solution)/shard_map/sub | solution.py:49
  217.8 12.3 %all-to-all-done.2 = f32[16,400,32]{1,2,0:T(8,128)} async-done(((f32[16,400,32]{1,2,0:T(8,128)}), f32[16,400,32]{1,2,0:T(8,128)}, u32[]{:S(2)}, u32[]{:S(2)}) %all-to-all-start.2) | async-done | bytes 819232 | tf_op jit(solution)/shard_map/all_to_all | solution.py:74
  230.1 2.0 stack.11
  232.1 4.4 %all-to-all-start.3 = ((f32[16,400,32]{1,2,0:T(8,128)}), f32[16,400,32]{1,2,0:T(8,128)}, u32[]{:S(2)}, u32[]{:S(2)}) async-start(f32[16,400,32]{1,2,0:T(8,128)} %stack.11), calls=%async_computation.5 | async-start | bytes 2097152 | tf_op jit(solution)/shard_map/all_to_all | solution.py:74
  236.5 2.4 copy.24
  238.9 1.7 multiply_convert_fusion.1
  240.6 4.0 fusion.5
  244.6 3.4 multiply_reduce_fusion.1
  248.0 2.3 fusion.18
  250.3 4.1 %all-to-all-done.3 = f32[16,400,32]{1,2,0:T(8,128)} async-done(((f32[16,400,32]{1,2,0:T(8,128)}), f32[16,400,32]{1,2,0:T(8,128)}, u32[]{:S(2)}, u32[]{:S(2)}) %all-to-all-start.3) | async-done | bytes 819232 | tf_op jit(solution)/shard_map/all_to_all | solution.py:74
  254.4 1.5 copy.25
  256.2 1.2 multiply_convert_fusion
  257.5 3.7 divide_subtract_fusion.1
  261.3 3.2 fusion.3
  264.6 1.3 copy-done.3
  265.9 2.3 fusion.14
  268.2 1.3 pad_maximum_fusion.2
  270.5 4.5 %multiply_reduce_fusion = (f32[2048]{0:T(1024)S(1)}, f32[400,2048]{1,0:T(8,128)}) fusion(bf16[400,512]{1,0:T(8,128)(2,1)} %copy-done.5, bf16[2048,512]{1,0:T(8,128)(2,1)} %copy-done.3), kind=kOutput, calls=%fused_computation.17 | convolution fusion | flops 840497152 | bytes 5791744 | tf_op jit(solution)/shard_map/dot_general | solution.py:83
  275.6 44.0 %reduce-scatter.9.cloned.1.call-done = f32[400,32]{0,1:T(8,128)} async-done(((f32[400,512]{0,1:T(8,128)}), f32[400,32]{0,1:T(8,128)}) %reduce-scatter.9.cloned.1.call-update) | async-done | bytes 51216 | tf_op jit(solution)/shard_map/reduce_scatter | solution.py:88
  319.6 2.3 multiply_reduce_fusion.5
  321.9 67.4 %reduce-scatter.11.cloned.1.call-done = f32[400,32]{0,1:T(8,128)} async-done(((f32[400,512]{0,1:T(8,128)}), f32[400,32]{0,1:T(8,128)}) %reduce-scatter.11.cloned.1.call-update) | async-done | bytes 51216 | tf_op jit(solution)/shard_map/reduce_scatter | solution.py:88
  389.3 1.2 multiply_reduce_fusion.4
  391.3 2.9 collective-permute-start.3
  396.1 4.3 %divide_subtract_fusion = f32[400,2048]{1,0:T(8,128)} fusion(f32[400,2048]{1,0:T(8,128)S(1)} %divide_subtract_fusion.1, f32[400,2048]{1,0:T(8,128)} %get-tuple-element.47, f32[2048]{0:T(1024)} %get-tuple-element.8), kind=kLoop, calls=%fused_computation.16 | loop fusion | flops 2457600 | bytes 9838592 | tf_op jit(solution)/shard_map/sub | solution.py:49
  (92 shorter events, 20.9 us)
Async XLA Ops:
  7.2 14.0 %copy-start = (f32[400,64]{0,1:T(8,128)S(1)}, f32[400,64]{0,1:T(8,128)}, u32[]{:S(2)}) copy-start(f32[400,64]{0,1:T(8,128)} %param.12) | copy-start | bytes 307204
  7.2 10.1 %copy-start.19 = (s32[2,2,16]{2,1,0:T(2,128)S(1)}, s32[2,2,16]{2,1,0:T(2,128)}, u32[]{:S(2)}) copy-start(s32[2,2,16]{2,1,0:T(2,128)} %param.15) | copy-start | bytes 772
  7.2 12.1 %copy-start.21 = (s32[2,2,16,4]{2,3,1,0:T(4,128)S(1)}, s32[2,2,16,4]{2,3,1,0:T(4,128)}, u32[]{:S(2)}) copy-start(s32[2,2,16,4]{2,3,1,0:T(4,128)} %param.14) | copy-start | bytes 3076
  7.2 12.3 %copy-start.20 = (s32[2,2,1,4]{3,2,1,0:T(1,128)S(1)}, s32[2,2,1,4]{3,2,1,0:T(1,128)}, u32[]{:S(2)}) copy-start(s32[2,2,1,4]{3,2,1,0:T(1,128)} %param.13) | copy-start | bytes 196
  9.2 26.0 %all-to-all-start = ((f32[16,400,32]{1,2,0:T(8,128)}), f32[16,400,32]{1,2,0:T(8,128)S(1)}, u32[]{:S(2)}, u32[]{:S(2)}) async-start(f32[16,400,32]{1,2,0:T(8,128)} %stack.8), calls=%async_computation | async-start | bytes 2097152 | tf_op jit(solution)/shard_map/all_to_all | solution.py:74
  17.3 54.5 %copy-start.15 = (s32[512]{0:T(512)}, s32[512]{0:T(512)S(1)}, u32[]{:S(2)}) copy-start(s32[512]{0:T(512)S(1)} %add_select_fusion) | copy-start | bytes 6148
  21.4 37.1 %copy-start.9 = (f32[4,400]{1,0:T(4,128)}, f32[4,400]{1,0:T(4,128)S(1)}, u32[]{:S(2)}) copy-start(f32[4,400]{1,0:T(4,128)S(1)} %fusion.32) | copy-start | bytes 19204
  21.6 21.4 %copy-start.10 = (f32[4,400]{1,0:T(4,128)}, f32[4,400]{1,0:T(4,128)S(1)}, u32[]{:S(2)}) copy-start(f32[4,400]{1,0:T(4,128)S(1)} %fusion.31) | copy-start | bytes 19204
  36.3 21.6 %all-to-all-start.1 = ((f32[16,400,32]{1,2,0:T(8,128)}), f32[16,400,32]{1,2,0:T(8,128)S(1)}, u32[]{:S(2)}, u32[]{:S(2)}) async-start(f32[16,400,32]{1,2,0:T(8,128)} %stack.9), calls=%async_computation.1 | async-start | bytes 2097152 | tf_op jit(solution)/shard_map/all_to_all | solution.py:74
  40.0 84.6 %reduce-scatter.5.cloned.1.call-start = ((), (), s32[]{:S(2)}) async-start(), calls=%async_computation.8 | async-start | bytes 1114112 | tf_op jit(solution)/shard_map/reduce_scatter | solution.py:88
  43.0 1.9 copy-start.6
  53.1 5.9 %copy-start.8 = (f32[2048]{0:T(1024)}, f32[2048]{0:T(1024)S(1)}, u32[]{:S(2)}) copy-start(f32[2048]{0:T(1024)S(1)} %get-tuple-element.36) | copy-start | bytes 24580
  55.4 3.7 copy-start.18
  58.3 136.8 %reduce-scatter.7.cloned.1.call-start = ((), (), s32[]{:S(2)}) async-start(), calls=%async_computation.9 | async-start | bytes 1114112 | tf_op jit(solution)/shard_map/reduce_scatter | solution.py:88
  59.1 3.8 copy-start.4
  66.1 1.3 copy-start.2
  67.4 130.2 %copy-start.7 = (f32[400,64]{0,1:T(8,128)S(1)}, f32[400,64]{0,1:T(8,128)}, u32[]{:S(2)}) copy-start(f32[400,64]{0,1:T(8,128)} %param.10) | copy-start | bytes 307204
  198.5 7.1 %collective-permute-start = (f32[400,64]{0,1:T(8,128)S(1)}, f32[400,64]{0,1:T(8,128)S(1)}, u32[]{:S(2)}, u32[]{:S(2)}) collective-permute-start(f32[400,64]{0,1:T(8,128)S(1)} %pad_maximum_fusion), channel_id=1, source_target_pairs={{0,16},{16,32},{32,48},{48,64},{64,80},{80,96},{96,112},{112,0},{1... | collective-permute-start | bytes 307208 | tf_op jit(solution)/shard_map/ppermute | solution.py:18
  207.4 22.7 %all-to-all-start.2 = ((f32[16,400,32]{1,2,0:T(8,128)}), f32[16,400,32]{1,2,0:T(8,128)}, u32[]{:S(2)}, u32[]{:S(2)}) async-start(f32[16,400,32]{1,2,0:T(8,128)} %stack.10), calls=%async_computation.4 | async-start | bytes 2097152 | tf_op jit(solution)/shard_map/all_to_all | solution.py:74
  217.8 22.8 %copy-start.1 = (f32[400,2048]{1,0:T(8,128)S(1)}, f32[400,2048]{1,0:T(8,128)}, u32[]{:S(2)}) copy-start(f32[400,2048]{1,0:T(8,128)} %divide_subtract_fusion.2) | copy-start | bytes 9830404
  232.1 22.3 %all-to-all-start.3 = ((f32[16,400,32]{1,2,0:T(8,128)}), f32[16,400,32]{1,2,0:T(8,128)}, u32[]{:S(2)}, u32[]{:S(2)}) async-start(f32[16,400,32]{1,2,0:T(8,128)} %stack.11), calls=%async_computation.5 | async-start | bytes 2097152 | tf_op jit(solution)/shard_map/all_to_all | solution.py:74
  236.5 83.2 %reduce-scatter.9.cloned.1.call-start = ((), (), s32[]{:S(2)}) async-start(), calls=%async_computation.10 | async-start | bytes 1114112 | tf_op jit(solution)/shard_map/reduce_scatter | solution.py:88
  250.3 7.2 %copy-start.11 = (f32[2048]{0:T(1024)S(1)}, f32[2048]{0:T(1024)}, u32[]{:S(2)}) copy-start(f32[2048]{0:T(1024)} %get-tuple-element.15) | copy-start | bytes 24580
  250.3 7.2 %copy-start.13 = (f32[2048]{0:T(1024)S(1)}, f32[2048]{0:T(1024)}, u32[]{:S(2)}) copy-start(f32[2048]{0:T(1024)} %get-tuple-element.44) | copy-start | bytes 24580
  256.0 133.3 %reduce-scatter.11.cloned.1.call-start = ((), (), s32[]{:S(2)}) async-start(), calls=%async_computation.11 | async-start | bytes 1114112 | tf_op jit(solution)/shard_map/reduce_scatter | solution.py:88
  257.5 3.8 copy-start.5
  257.5 3.8 copy-start.16
  257.5 3.8 copy-start.17
  264.5 1.3 copy-start.3
  269.6 5.5 %copy-start.12 = (f32[2048]{0:T(1024)S(1)}, f32[2048]{0:T(1024)}, u32[]{:S(2)}) copy-start(f32[2048]{0:T(1024)} %get-tuple-element.15) | copy-start | bytes 24580
  269.6 5.5 %copy-start.14 = (f32[2048]{0:T(1024)S(1)}, f32[2048]{0:T(1024)}, u32[]{:S(2)}) copy-start(f32[2048]{0:T(1024)} %get-tuple-element.44) | copy-start | bytes 24580
  269.6 120.9 %collective-permute-start.1 = (f32[64]{0:T(128)}, f32[64]{0:T(128)}, u32[]{:S(2)}, u32[]{:S(2)}) collective-permute-start(f32[64]{0:T(128)} %pad_maximum_fusion.2), channel_id=1, source_target_pairs={{0,16},{16,32},{32,48},{48,64},{64,80},{80,96},{96,112},{112,0},{1... | collective-permute-start | bytes 776 | tf_op jit(solution)/shard_map/ppermute | solution.py:18
  391.3 9.1 %collective-permute-start.3 = (f32[64]{0:T(128)S(1)}, f32[64]{0:T(128)S(1)}, u32[]{:S(2)}, u32[]{:S(2)}) collective-permute-start(f32[64]{0:T(128)S(1)} %pad_maximum_fusion.3), channel_id=1, source_target_pairs={{0,112},{16,0},{32,16},{48,32},{64,48},{80,64},{96,80},{112,96},{1... | collective-permute-start | bytes 776 | tf_op jit(solution)/shard_map/ppermute | solution.py:18
  395.2 5.3 %collective-permute-start.2 = (f32[400,64]{0,1:T(8,128)S(1)}, f32[400,64]{0,1:T(8,128)S(1)}, u32[]{:S(2)}, u32[]{:S(2)}) collective-permute-start(f32[400,64]{0,1:T(8,128)S(1)} %pad_maximum_fusion.1), channel_id=1, source_target_pairs={{0,112},{16,0},{32,16},{48,32},{64,48},{80,64},{96,80},{112,96},{1... | collective-permute-start | bytes 307208 | tf_op jit(solution)/shard_map/ppermute | solution.py:18
Sparse Core Ops, SparseCore 0:
  58.4 66.2 reduce-scatter.4
  129.0 65.9 reduce-scatter.6
  256.1 63.4 reduce-scatter.8
  323.3 65.9 reduce-scatter.10
